TPU v7x, 256 devices: a whole 4x4x8 slice. The times are simulated.
256 devices in a mesh: head: 4 (over x), blk: 64 (over y, z, core).
Axes of the slice: x: 4, y: 4, z: 8, core: 2. Of those that a mesh axis runs over, the one named last changes fastest.
Arguments:
- doc_x: bfloat16 [65536, 1024], P('blk'), may hold values from -6 to 6
- doc_seg: int32 [65536], P('blk'), may hold values from 0 to 1023, as said below
- doc_query: int32 [1024], replicated, may hold values from 0 to 7
- doc_var: int32 [65536], P('blk'), may hold values from 0 to 7
- query_len: int32 [8], replicated, may hold values from 256 to 4096, as said below
- block_perm: int32 [64], replicated, may hold values from 0 to 63, each once
- cache_k: bfloat16 [32768, 1024], P('blk', 'head'), may hold values from -164 to 164
- cache_v: bfloat16 [32768, 1024], P('blk', 'head'), may hold values from -6 to 6
- cache_var: int32 [32768], P('blk'), may hold values from 0 to 7
- w_query: bfloat16 [1024, 1024], P(None, 'head'), may hold values from -0.1875 to 0.1875
- w_key: bfloat16 [1024, 1024], P(None, 'head'), may hold values from -0.5 to 0.5
- w_value: bfloat16 [1024, 1024], P(None, 'head'), may hold values from -0.1875 to 0.1875
- w_out: bfloat16 [1024, 1024], P('head'), may hold values from -0.1875 to 0.1875
- var_bias: float32 [2, 16], P(None, 'head'), may hold values from -1 to 1
- norm_gain: float32 [1024], replicated, may hold values from 0.1 to 1.9
- readout: float32 [1024], replicated, may hold values from -1.5 to 1.5
Outputs:
- update: float32 [65536, 1024], P('blk', 'head')
- pooled: float32 [1024], P('blk')
Inputs may be any that keep to these rules, and one draw needn't show every extreme that they name: `doc_seg`: index i of blk holds documents i * 16 to (i + 1) * 16 - 1 whole; its 1024 tokens form 8 runs of 128 tokens, run j holding its documents 2j and 2j + 1, both of one query, and the 8 runs of one index belong to 8 different queries. query_len[0] = 4096.
All inputs are finite; a program needn't handle non-finite values.
Results may differ from a plain program's by a relative error of at most 0.012.
The roundings to bfloat16 on the way count: a program that leaves them out, or rounds other values in their place, can miss the bound.
Values may be sent and summed in bfloat16 or wider, within the bound.
A program may use at most 128 MiB of HBM per device.

v0:
```python
import jax
import jax.numpy as jnp
from jax import lax
from jax.sharding import PartitionSpec as P

D = 1024
DH = 64
QUERIES = 8


def rotary(projected, positions):
    row_count = projected.shape[0]
    head_count = projected.shape[1] // DH
    half_size = DH // 2
    shaped = projected.reshape(row_count, head_count, DH)
    frequency = 10000.0 ** (-jnp.arange(half_size, dtype=jnp.float32) / half_size)
    angles = positions.astype(jnp.float32)[:, None] * frequency[None, :]
    cosine = jnp.cos(angles)[:, None, :]
    sine_part = jnp.sin(angles)[:, None, :]
    first_half = shaped[:, :, :half_size]
    second_half = shaped[:, :, half_size:]
    turned = jnp.concatenate(
        [
            first_half * cosine - second_half * sine_part,
            second_half * cosine + first_half * sine_part,
        ],
        axis=2,
    )
    return turned.reshape(row_count, head_count * DH)


def softmax_part(scores, allowed):
    scores = jnp.where(allowed, scores, -1e30)
    peak = jnp.max(scores, axis=-1)
    weights = jnp.where(allowed, jnp.exp(scores - peak[..., None]), 0.0)
    return (peak, jnp.sum(weights, axis=-1), weights.astype(jnp.bfloat16))


def cache_part(
    recv_q, recv_var, cache_keys, cache_values, cache_var, row_valid, bias_same, bias_other
):
    source_count = recv_q.shape[0]
    item_count = recv_q.shape[1]
    col_count = recv_q.shape[2]
    head_count = cache_keys.shape[1]
    total_rows = source_count * item_count
    block_rows = 512
    block_count = total_rows // block_rows
    flat_q = recv_q.reshape(block_count, block_rows, head_count, DH)
    flat_var = recv_var.reshape(block_count, block_rows).astype(jnp.int32)

    def one_block(block_inputs):
        block_q, block_var = block_inputs
        scores = (
            jnp.einsum("thd,rhd->htr", block_q, cache_keys, preferred_element_type=jnp.float32)
            * 0.125
        )
        scores = scores + jnp.where(
            (block_var[:, None] == cache_var[None, :])[None], bias_same, bias_other
        )
        allowed = jnp.broadcast_to(row_valid[None, None, :], scores.shape)
        peak, total_weight, weights = softmax_part(scores, allowed)
        mixed = jnp.einsum(
            "htr,rhd->thd", weights, cache_values, preferred_element_type=jnp.float32
        )
        return (peak.T, total_weight.T, mixed.reshape(block_rows, col_count))

    maxima, totals, sums = lax.map(one_block, (flat_q, flat_var))
    return (
        maxima.reshape(source_count, item_count, head_count),
        totals.reshape(source_count, item_count, head_count),
        sums.reshape(source_count, item_count, col_count),
    )


def body(
    doc_x,
    doc_seg,
    doc_query,
    doc_var,
    query_len,
    block_perm,
    cache_k,
    cache_v,
    cache_var,
    w_query,
    w_key,
    w_value,
    w_out,
    var_bias,
    norm_gain,
    readout,
):
    row_count = doc_x.shape[0]
    col_count = w_query.shape[1]
    head_count = col_count // DH
    cache_count = cache_k.shape[0]
    blk_count = lax.axis_size("blk")
    blk_index = lax.axis_index("blk")
    head_index = lax.axis_index("head")
    blocks_each = blk_count // QUERIES
    slot_count = QUERIES
    slot_rows = row_count // slot_count
    doc_count = 2 * slot_count
    first_doc = blk_index * doc_count
    local_seg = doc_seg - first_doc
    member = (local_seg[:, None] == jnp.arange(doc_count, dtype=jnp.int32)[None, :]).astype(
        jnp.int32
    )
    lengths = jnp.sum(member, axis=0)
    starts = jnp.cumsum(lengths) - lengths
    first_pos = jnp.dot(member, starts)
    own_docs_query = lax.dynamic_slice_in_dim(doc_query, first_doc, doc_count)
    query_table = (own_docs_query[:, None] == jnp.arange(QUERIES, dtype=jnp.int32)[None, :]).astype(
        jnp.int32
    )
    doc_len = jnp.sum(query_table * query_len[None, :], axis=1)
    tok_len = jnp.dot(member, doc_len)
    positions = tok_len + jnp.arange(row_count, dtype=jnp.int32) - first_pos
    query_rot = rotary(
        jnp.dot(doc_x, w_query, preferred_element_type=jnp.float32), positions
    ).astype(jnp.bfloat16)
    key_rot = rotary(jnp.dot(doc_x, w_key, preferred_element_type=jnp.float32), positions).astype(
        jnp.bfloat16
    )
    value_proj = jnp.dot(doc_x, w_value, preferred_element_type=jnp.float32).astype(jnp.bfloat16)
    bias_same = var_bias[0][:, None, None]
    bias_other = var_bias[1][:, None, None]
    shaped_q = query_rot.reshape(slot_count, slot_rows, head_count, DH)
    shaped_k = key_rot.reshape(slot_count, slot_rows, head_count, DH)
    shaped_v = value_proj.reshape(slot_count, slot_rows, head_count, DH)
    slot_seg = local_seg.reshape(slot_count, slot_rows)
    slot_var = doc_var.reshape(slot_count, slot_rows)
    self_scores = (
        jnp.einsum("gthd,gshd->ghts", shaped_q, shaped_k, preferred_element_type=jnp.float32)
        * 0.125
    )
    self_scores = self_scores + jnp.where(
        (slot_var[:, :, None] == slot_var[:, None, :])[:, None], bias_same[None], bias_other[None]
    )
    self_allowed = (slot_seg[:, :, None] == slot_seg[:, None, :])[:, None]
    self_peak, self_total, self_weights = softmax_part(self_scores, self_allowed)
    self_sum = jnp.einsum(
        "ghts,gshd->gthd", self_weights, shaped_v, preferred_element_type=jnp.float32
    )
    self_peak = self_peak.transpose(0, 2, 1)
    self_total = self_total.transpose(0, 2, 1)
    slot_query = own_docs_query.reshape(slot_count, 2)[:, 0]
    block_query = block_perm // blocks_each
    slot_match = block_query[:, None] == slot_query[None, :]
    slot_pick = jnp.sum(
        slot_match.astype(jnp.int32) * jnp.arange(slot_count, dtype=jnp.int32)[None, :], axis=1
    )
    send_q = jnp.take(query_rot.reshape(slot_count, slot_rows, col_count), slot_pick, axis=0)
    send_var = jnp.take(slot_var, slot_pick, axis=0).astype(jnp.bfloat16)
    my_block = lax.dynamic_slice_in_dim(block_perm, blk_index, 1)[0]
    my_query = my_block // blocks_each
    first_row = my_block % blocks_each * cache_count
    my_len = lax.dynamic_slice_in_dim(query_len, my_query, 1)[0]
    row_valid = first_row + jnp.arange(cache_count, dtype=jnp.int32) < my_len
    cache_keys = cache_k.reshape(cache_count, head_count, DH)
    cache_values = cache_v.reshape(cache_count, head_count, DH)
    recv_q, recv_var = (
        lax.all_to_all(send_q, "blk", split_axis=0, concat_axis=0, tiled=True),
        lax.all_to_all(send_var, "blk", split_axis=0, concat_axis=0, tiled=True),
    )
    maxima, totals, sums = cache_part(
        recv_q, recv_var, cache_keys, cache_values, cache_var, row_valid, bias_same, bias_other
    )
    got_max, got_total, got_sum = (
        lax.all_to_all(maxima, "blk", split_axis=0, concat_axis=0, tiled=True),
        lax.all_to_all(totals, "blk", split_axis=0, concat_axis=0, tiled=True),
        lax.all_to_all(sums, "blk", split_axis=0, concat_axis=0, tiled=True),
    )
    match_float = slot_match.astype(jnp.float32)
    spread_max = jnp.where(slot_match[:, :, None, None], got_max[:, None], -1e30)
    cache_peak = jnp.max(spread_max, axis=0)
    peak = jnp.maximum(cache_peak, self_peak)
    device_peak = jnp.take(peak, slot_pick, axis=0)
    factor = jnp.exp(got_max - device_peak)
    cache_total = jnp.einsum(
        "dg,dth->gth", match_float, got_total * factor, precision=lax.Precision.HIGHEST
    )
    scaled_sum = got_sum.reshape(blk_count, slot_rows, head_count, DH) * factor[..., None]
    cache_sum = jnp.einsum(
        "dg,dthe->gthe", match_float, scaled_sum, precision=lax.Precision.HIGHEST
    )
    self_factor = jnp.exp(self_peak - peak)
    numerator = cache_sum + self_sum * self_factor[..., None]
    denominator = cache_total + self_total * self_factor
    attended = (
        (numerator / denominator[..., None]).reshape(row_count, col_count).astype(jnp.bfloat16)
    )
    partial_update = jnp.dot(attended, w_out, preferred_element_type=jnp.float32)
    x_float = doc_x.astype(jnp.float32)
    whole_sum = lax.psum(partial_update, "head")
    hidden = x_float + whole_sum
    square_sum = jnp.sum(hidden * hidden, axis=1)
    weighted = jnp.sum(hidden * norm_gain * readout, axis=1)
    update = lax.dynamic_slice_in_dim(whole_sum, head_index * col_count, col_count, 1)
    token_score = weighted * lax.rsqrt(square_sum / D + 1e-06)
    pooled_sum = jnp.dot(token_score, member.astype(jnp.float32), precision=lax.Precision.HIGHEST)
    return (update, pooled_sum / lengths.astype(jnp.float32))


def solution(mesh):
    return jax.shard_map(
        body,
        mesh=mesh,
        in_specs=(
            P("blk", None),
            P("blk"),
            P(),
            P("blk"),
            P(),
            P(),
            P("blk", "head"),
            P("blk", "head"),
            P("blk"),
            P(None, "head"),
            P(None, "head"),
            P(None, "head"),
            P("head", None),
            P(None, "head"),
            P(),
            P(),
        ),
        out_specs=(P("blk", "head"), P("blk")),
        check_vma=False,
    )
```

profile of v0, /device:TPU:1, one launch (start us, length us, event | category | flops | bytes accessed | tf_op | source)
XLA Modules:
  0.0 646.7 jit_solution(2000789111802115484)
XLA Ops:
  11.0 13.2 %all-to-all-start.1 = ((bf16[64,1,128]{2,1,0:T(2,128)(2,1)}), bf16[64,1,128]{2,1,0:T(2,128)(2,1)S(1)}, u32[]{:S(2)}, u32[]{:S(2)}) async-start(bf16[64,1,128]{2,1,0:T(2,128)(2,1)} %copy.100), calls=%async_computation.1 | async-start | bytes 65536 | tf_op jit(solution)/shard_map/all_to_all | solution.py:165
  30.1 2.8 gather_fusion
  32.8 4.6 broadcast_select_fusion
  37.4 10.7 %all-to-all-start = ((bf16[64,128,256]{2,1,0:T(8,128)(2,1)}), bf16[64,128,256]{2,1,0:T(8,128)(2,1)}, u32[]{:S(2)}, u32[]{:S(2)}) async-start(bf16[64,128,256]{2,1,0:T(8,128)(2,1)} %broadcast_select_fusion), calls=%async_computation | async-start | bytes 8388608 | tf_op jit(solution)/shard_map/all_to_all | solution.py:164
  53.1 90.9 %all-to-all-done = bf16[64,128,256]{2,1,0:T(8,128)(2,1)} async-done(((bf16[64,128,256]{2,1,0:T(8,128)(2,1)}), bf16[64,128,256]{2,1,0:T(8,128)(2,1)}, u32[]{:S(2)}, u32[]{:S(2)}) %all-to-all-start) | async-done | bytes 4194336 | tf_op jit(solution)/shard_map/all_to_all | solution.py:164
  144.0 12.9 %reshape.307 = bf16[16,512,4,64]{3,2,1,0:T(4,128)(2,1)} reshape(bf16[64,128,256]{2,1,0:T(8,128)(2,1)} %all-to-all-done) | data formatting | bytes 8388608 | tf_op jit(solution)/shard_map/reshape | solution.py:49
  156.9 12.7 %copy.102 = bf16[16,512,4,64]{1,3,2,0:T(8,128)(2,1)} copy(bf16[16,512,4,64]{3,2,1,0:T(4,128)(2,1)} %reshape.307) | data formatting | bytes 8388608
  169.6 122.0 %while.15 = (s32[]{:T(128)}, f32[16,512,4]{1,2,0:T(4,128)S(1)}, f32[16,512,4]{1,2,0:T(4,128)S(1)}, f32[16,512,256]{2,1,0:T(8,128)}, bf16[16,512,4,64]{1,3,2,0:T(...) while((s32[]{:T(128)}, f32[16,512,4]{1,2,0:T(4,128)S(1)}, ...), condition=%wide.region_7.8_spmd.clone, body=%wide.region_4.7_spmd.clone.sunk | while | flops 288617472 | bytes 17115396 | solution.py:68
  193.5 2.5 fusion.87
  208.7 2.5 fusion.87
  216.3 2.5 fusion.87
  246.8 2.5 fusion.87
  291.6 16.0 %all_to_all.26 = f32[64,128,4]{1,2,0:T(4,128)} all-to-all(f32[64,128,4]{1,2,0:T(4,128)S(1)} %bitcast.155), channel_id=1, replica_groups=mesh['head'=4,'blk'=64] {'blk'}, dimensions={0} | all-to-all | bytes 262144 | tf_op jit(solution)/shard_map/all_to_all | solution.py:172
  307.6 15.0 %all_to_all.27 = f32[64,128,4]{1,2,0:T(4,128)S(1)} all-to-all(f32[64,128,4]{1,2,0:T(4,128)S(1)} %bitcast.154), channel_id=1, replica_groups=mesh['head'=4,'blk'=64] {'blk'}, dimensions={0} | all-to-all | bytes 262144 | tf_op jit(solution)/shard_map/all_to_all | solution.py:171
  322.6 5.6 all-to-all-start.2
  330.0 2.5 convolution_convert_fusion
  332.5 2.8 reshape.308
  342.1 172.0 %all-to-all-done.2 = f32[64,128,256]{2,1,0:T(8,128)} async-done(((f32[64,128,256]{2,1,0:T(8,128)}), f32[64,128,256]{2,1,0:T(8,128)}, u32[]{:S(2)}, u32[]{:S(2)}) %all-to-all-start.2) | async-done | bytes 8388640 | tf_op jit(solution)/shard_map/all_to_all | solution.py:173
  514.1 9.0 %copy.104 = f32[64,128,256]{1,2,0:T(8,128)} copy(f32[64,128,256]{2,1,0:T(8,128)} %all-to-all-done.2) | data formatting | bytes 16777216 | tf_op jit(solution)/shard_map/all_to_all | solution.py:173
  523.0 4.6 broadcast_multiply_fusion
  527.7 8.5 %fusion.24 = bf16[8,128,4,64]{1,0,3,2:T(8,128)(2,1)S(1)} fusion(f32[64,128,4,64]{1,3,2,0:T(8,128)S(1)} %broadcast_multiply_fusion, f32[8,4,64,128]{3,2,1,0:T(8,128)S(1)} %copy-done.3, f32[8,128,4]{1,0,2:T(8,128)S(1)} %convolution_add_fusion, f32[8,128,4]{1,0,2:T(8,128)S(1)} %get-tuple-element.189, s32[64]{0:T(128)S(1)} %copy-done.16, s32[8]{0:T(128)S(1)} %copy-done.13), kind=kOutput, calls=%fused_computation.36 | convolution fusion | flops 202375680 | bytes 9994528 | tf_op jit(solution)/shard_map/dg,dthe->gthe/dot_general | solution.py:185
  536.2 2.7 fusion.34
  539.0 94.6 %all-reduce.2.cloned.1.call-done = f32[1024,1024]{1,0:T(8,128)} async-done(((f32[1024,1024]{1,0:T(8,128)}), f32[1024,1024]{1,0:T(8,128)}) %all-reduce.2.cloned.1.call-update) | async-done | bytes 4194320 | tf_op jit(solution)/shard_map/psum | solution.py:196
  633.6 3.3 multiply_reduce_fusion
  (255 shorter events, 134.7 us)
Async XLA Ops:
  7.2 529.0 %copy-start = (bf16[256,1024]{1,0:T(8,128)(2,1)S(1)}, bf16[256,1024]{1,0:T(8,128)(2,1)}, u32[]{:S(2)}) copy-start(bf16[256,1024]{1,0:T(8,128)(2,1)} %param.30) | copy-start | bytes 1572868
  7.9 320.7 %copy-start.15 = (s32[64]{0:T(128)}, s32[64]{0:T(128)S(1)}, u32[]{:S(2)}) copy-start(s32[64]{0:T(128)S(1)} %and_select_fusion) | copy-start | bytes 772
  8.9 319.7 %copy-start.12 = (s32[8]{0:T(128)}, s32[8]{0:T(128)S(1)}, u32[]{:S(2)}) copy-start(s32[8]{0:T(128)S(1)} %slice_reduce_fusion) | copy-start | bytes 100
  9.0 23.9 %copy-start.17 = (pred[64]{0:T(512)(128)(4,1)}, pred[64]{0:T(512)(128)(4,1)S(1)}, u32[]{:S(2)}) copy-start(pred[64]{0:T(512)(128)(4,1)S(1)} %compare_and_fusion) | copy-start | bytes 196
  9.0 21.1 %copy-start.14 = (s32[1024]{0:T(1024)}, s32[1024]{0:T(1024)S(1)}, u32[]{:S(2)}) copy-start(s32[1024]{0:T(1024)S(1)} %pad_clamp_fusion) | copy-start | bytes 12292
  11.0 26.4 %all-to-all-start.1 = ((bf16[64,1,128]{2,1,0:T(2,128)(2,1)}), bf16[64,1,128]{2,1,0:T(2,128)(2,1)S(1)}, u32[]{:S(2)}, u32[]{:S(2)}) async-start(bf16[64,1,128]{2,1,0:T(2,128)(2,1)} %copy.100), calls=%async_computation.1 | async-start | bytes 65536 | tf_op jit(solution)/shard_map/all_to_all | solution.py:165
  24.9 4.8 copy-start.10
  37.4 10.7 %copy-start.26 = (s32[64]{0:T(128)S(1)}, s32[64]{0:T(128)}, u32[]{:S(2)}) copy-start(s32[64]{0:T(128)} %param.23) | copy-start | bytes 772
  37.4 13.9 %copy-start.6 = (bf16[512,256]{1,0:T(8,128)(2,1)S(1)}, bf16[512,256]{1,0:T(8,128)(2,1)}, u32[]{:S(2)}) copy-start(bf16[512,256]{1,0:T(8,128)(2,1)} %param.24) | copy-start | bytes 786436
  37.4 14.1 %copy-start.7 = (bf16[512,256]{1,0:T(8,128)(2,1)S(1)}, bf16[512,256]{1,0:T(8,128)(2,1)}, u32[]{:S(2)}) copy-start(bf16[512,256]{1,0:T(8,128)(2,1)} %param.25) | copy-start | bytes 786436
  37.4 14.3 %copy-start.27 = (s32[8]{0:T(128)S(1)}, s32[8]{0:T(128)}, u32[]{:S(2)}) copy-start(s32[8]{0:T(128)} %param.22) | copy-start | bytes 100
  37.4 14.9 %copy-start.23 = (f32[2,4]{1,0:T(2,128)S(1)}, f32[2,4]{1,0:T(2,128)}, u32[]{:S(2)}) copy-start(f32[2,4]{1,0:T(2,128)} %param.31) | copy-start | bytes 100
  37.4 106.5 %all-to-all-start = ((bf16[64,128,256]{2,1,0:T(8,128)(2,1)}), bf16[64,128,256]{2,1,0:T(8,128)(2,1)}, u32[]{:S(2)}, u32[]{:S(2)}) async-start(bf16[64,128,256]{2,1,0:T(8,128)(2,1)} %broadcast_select_fusion), calls=%async_computation | async-start | bytes 8388608 | tf_op jit(solution)/shard_map/all_to_all | solution.py:164
  156.9 12.7 %copy-start.8 = (s32[512]{0:T(512)S(1)}, s32[512]{0:T(512)}, u32[]{:S(2)}) copy-start(s32[512]{0:T(512)} %param.26) | copy-start | bytes 6148
  322.6 7.4 %copy-start.1 = (bf16[1024,1024]{1,0:T(8,128)(2,1)S(1)}, bf16[1024,1024]{1,0:T(8,128)(2,1)}, u32[]{:S(2)}) copy-start(bf16[1024,1024]{1,0:T(8,128)(2,1)} %param.18) | copy-start | bytes 6291460
  322.6 191.5 %all-to-all-start.2 = ((f32[64,128,256]{2,1,0:T(8,128)}), f32[64,128,256]{2,1,0:T(8,128)}, u32[]{:S(2)}, u32[]{:S(2)}) async-start(f32[64,128,256]{2,1,0:T(8,128)} %bitcast.145), calls=%async_computation.2 | async-start | bytes 16777216 | tf_op jit(solution)/shard_map/all_to_all | solution.py:173
  328.3 7.0 %copy-start.9 = (s32[1024]{0:T(1024)S(1)}, s32[1024]{0:T(1024)}, u32[]{:S(2)}) copy-start(s32[1024]{0:T(1024)} %param.19) | copy-start | bytes 12292
  328.3 7.0 %copy-start.2 = (s32[1024]{0:T(1024)S(1)}, s32[1024]{0:T(1024)}, u32[]{:S(2)}) copy-start(s32[1024]{0:T(1024)} %param.21) | copy-start | bytes 12292
  328.3 305.3 %all-reduce.2.cloned.1.call-start = ((), (), s32[]{:S(2)}) async-start(), calls=%async_computation.5 | async-start | bytes 8388608 | tf_op jit(solution)/shard_map/psum | solution.py:196
  523.0 4.7 copy-start.3
  538.9 94.7 %copy-start.19 = (f32[1024]{0:T(1024)S(1)}, f32[1024]{0:T(1024)}, u32[]{:S(2)}) copy-start(f32[1024]{0:T(1024)} %param.33) | copy-start | bytes 12292
  538.9 94.7 %copy-start.20 = (f32[1024]{0:T(1024)S(1)}, f32[1024]{0:T(1024)}, u32[]{:S(2)}) copy-start(f32[1024]{0:T(1024)} %param.32) | copy-start | bytes 12292
  539.0 97.9 %copy-start.11 = (s32[1024]{0:T(1024)S(1)}, s32[1024]{0:T(1024)}, u32[]{:S(2)}) copy-start(s32[1024]{0:T(1024)} %copy-done.10) | copy-start | bytes 12292
  539.0 97.9 %copy-start.22 = (s32[16]{0:T(128)S(1)}, s32[16]{0:T(128)}, u32[]{:S(2)}) copy-start(s32[16]{0:T(128)} %copy-done.21) | copy-start | bytes 196
  (8 other events, 10.8 us)
Sparse Core Ops, SparseCore 0:
  539.1 94.4 all-reduce.1
where the time goes:
time: 649 us; the launch traced here: 647 us
  waiting for transfers between devices  358 us (55%)
  matrix products  87.6 us (13%)
  local copies, waits for them, and re-layouts  66.9 us (10%)
  other arithmetic  56 us (9%)
  blocking collectives  31 us (5%)
  starting transfers between devices  29.7 us (5%)
  between operations  17.2 us (3%)
    all_to_all x1, waiting for transfers between devices, body(): lax.all_to_all(sums, 'blk', split_axis=0, concat_axis=0, tiled=True)  172 us
    psum x1, waiting for transfers between devices, body(): whole_sum = lax.psum(partial_update, 'head')  94.6 us
    all_to_all x1, waiting for transfers between devices, body(): lax.all_to_all(send_q, 'blk', split_axis=0, concat_axis=0, tiled=True)  90.9 us
    dot_general x16, matrix products, one_block(): jnp.einsum('thd,rhd->htr', block_q, cache_keys, preferred_element_type=jn...  39.2 us
    dot_general x16, matrix products, one_block(): jnp.einsum('htr,rhd->thd', weights, cache_values, preferred_element_type=...  26.9 us
    reduce_sum x17, other arithmetic, softmax_part(): return (peak, jnp.sum(weights, axis=-1), weights.astype(jnp.bfloat16))  24 us
    dynamic_update_slice x48, local copies, waits for them, and re-layouts, cache_part(): maxima, totals, sums = lax.map(one_block, (flat_q, flat_var))  16.9 us
    all_to_all x1, blocking collectives, body(): lax.all_to_all(totals, 'blk', split_axis=0, concat_axis=0, tiled=True)  16 us
  transfers between devices with their start and end apart: 4, of which 3 were waited for; matrix products, arithmetic and copies ran while one was open for 4% of the time, Pallas kernels for 0%

commit v1 on v0

--- a/solution.py
+++ b/solution.py
@@ -193,7 +193,8 @@
     )
     partial_update = jnp.dot(attended, w_out, preferred_element_type=jnp.float32)
     x_float = doc_x.astype(jnp.float32)
-    whole_sum = lax.psum(partial_update, "head")
+    blocks = lax.all_gather(partial_update, "head", axis=0, tiled=False)
+    whole_sum = blocks.sum(axis=0)
     hidden = x_float + whole_sum
     square_sum = jnp.sum(hidden * hidden, axis=1)
     weighted = jnp.sum(hidden * norm_gain * readout, axis=1)

time: 649 us -> 718 us (1.11)
  waiting for transfers between devices: 358 us -> 416 us
  other arithmetic: 56 us -> 66.5 us
    all_gather x0 -> x1, waiting for transfers between devices: none -> 153 us  [body(): blocks = lax.all_gather(partial_update, 'head', axis=0, tiled=False)]
    psum x1 -> x0, waiting for transfers between devices: 94.6 us -> none  [body(): whole_sum = lax.psum(partial_update, 'head')]
    reduce_sum x0 -> x1, other arithmetic: none -> 10.5 us  [body(): whole_sum = blocks.sum(axis=0)]
where the time goes in v1:
time: 718 us; the launch traced here: 716 us
  waiting for transfers between devices  416 us (58%)
  matrix products  87.6 us (12%)
  local copies, waits for them, and re-layouts  66.9 us (9%)
  other arithmetic  66.5 us (9%)
  blocking collectives  31 us (4%)
  starting transfers between devices  29.7 us (4%)
  between operations  17.2 us (2%)
    all_to_all x1, waiting for transfers between devices, body(): lax.all_to_all(sums, 'blk', split_axis=0, concat_axis=0, tiled=True)  172 us
    all_gather x1, waiting for transfers between devices, body(): blocks = lax.all_gather(partial_update, 'head', axis=0, tiled=False)  153 us
    all_to_all x1, waiting for transfers between devices, body(): lax.all_to_all(send_q, 'blk', split_axis=0, concat_axis=0, tiled=True)  90.9 us
    dot_general x16, matrix products, one_block(): jnp.einsum('thd,rhd->htr', block_q, cache_keys, preferred_element_type=jn...  39.2 us
    dot_general x16, matrix products, one_block(): jnp.einsum('htr,rhd->thd', weights, cache_values, preferred_element_type=...  26.9 us
    reduce_sum x17, other arithmetic, softmax_part(): return (peak, jnp.sum(weights, axis=-1), weights.astype(jnp.bfloat16))  24 us
    dynamic_update_slice x48, local copies, waits for them, and re-layouts, cache_part(): maxima, totals, sums = lax.map(one_block, (flat_q, flat_var))  16.9 us
    all_to_all x1, blocking collectives, body(): lax.all_to_all(totals, 'blk', split_axis=0, concat_axis=0, tiled=True)  16 us
  transfers between devices with their start and end apart: 4, of which 3 were waited for; matrix products, arithmetic and copies ran while one was open for 4% of the time, Pallas kernels for 0%

profile of v1, /device:TPU:1, one launch (start us, length us, event | category | flops | bytes accessed | tf_op | source)
XLA Modules:
  0.0 716.0 jit_solution(9885027906692869637)
XLA Ops:
  11.0 13.2 %all-to-all-start.1 = ((bf16[64,1,128]{2,1,0:T(2,128)(2,1)}), bf16[64,1,128]{2,1,0:T(2,128)(2,1)S(1)}, u32[]{:S(2)}, u32[]{:S(2)}) async-start(bf16[64,1,128]{2,1,0:T(2,128)(2,1)} %copy.100), calls=%async_computation.1 | async-start | bytes 65536 | tf_op jit(solution)/shard_map/all_to_all | solution.py:165
  30.1 2.8 gather_fusion
  32.8 4.6 broadcast_select_fusion
  37.4 10.7 %all-to-all-start = ((bf16[64,128,256]{2,1,0:T(8,128)(2,1)}), bf16[64,128,256]{2,1,0:T(8,128)(2,1)}, u32[]{:S(2)}, u32[]{:S(2)}) async-start(bf16[64,128,256]{2,1,0:T(8,128)(2,1)} %broadcast_select_fusion), calls=%async_computation | async-start | bytes 8388608 | tf_op jit(solution)/shard_map/all_to_all | solution.py:164
  53.1 90.9 %all-to-all-done = bf16[64,128,256]{2,1,0:T(8,128)(2,1)} async-done(((bf16[64,128,256]{2,1,0:T(8,128)(2,1)}), bf16[64,128,256]{2,1,0:T(8,128)(2,1)}, u32[]{:S(2)}, u32[]{:S(2)}) %all-to-all-start) | async-done | bytes 4194336 | tf_op jit(solution)/shard_map/all_to_all | solution.py:164
  144.0 12.9 %reshape.308 = bf16[16,512,4,64]{3,2,1,0:T(4,128)(2,1)} reshape(bf16[64,128,256]{2,1,0:T(8,128)(2,1)} %all-to-all-done) | data formatting | bytes 8388608 | tf_op jit(solution)/shard_map/reshape | solution.py:49
  156.9 12.7 %copy.102 = bf16[16,512,4,64]{1,3,2,0:T(8,128)(2,1)} copy(bf16[16,512,4,64]{3,2,1,0:T(4,128)(2,1)} %reshape.308) | data formatting | bytes 8388608
  169.6 122.0 %while.15 = (s32[]{:T(128)}, f32[16,512,4]{1,2,0:T(4,128)S(1)}, f32[16,512,4]{1,2,0:T(4,128)S(1)}, f32[16,512,256]{2,1,0:T(8,128)}, bf16[16,512,4,64]{1,3,2,0:T(...) while((s32[]{:T(128)}, f32[16,512,4]{1,2,0:T(4,128)S(1)}, ...), condition=%wide.region_7.8_spmd.clone, body=%wide.region_4.7_spmd.clone.sunk | while | flops 288617472 | bytes 17115396 | solution.py:68
  193.5 2.5 fusion.87
  208.7 2.5 fusion.87
  246.8 2.5 fusion.87
  291.6 16.0 %all_to_all.26 = f32[64,128,4]{1,2,0:T(4,128)} all-to-all(f32[64,128,4]{1,2,0:T(4,128)S(1)} %bitcast.157), channel_id=1, replica_groups=mesh['head'=4,'blk'=64] {'blk'}, dimensions={0} | all-to-all | bytes 262144 | tf_op jit(solution)/shard_map/all_to_all | solution.py:172
  307.6 15.0 %all_to_all.27 = f32[64,128,4]{1,2,0:T(4,128)S(1)} all-to-all(f32[64,128,4]{1,2,0:T(4,128)S(1)} %bitcast.156), channel_id=1, replica_groups=mesh['head'=4,'blk'=64] {'blk'}, dimensions={0} | all-to-all | bytes 262144 | tf_op jit(solution)/shard_map/all_to_all | solution.py:171
  322.6 5.6 all-to-all-start.2
  330.0 2.5 convolution_convert_fusion
  332.5 2.8 reshape.309
  342.1 172.0 %all-to-all-done.2 = f32[64,128,256]{2,1,0:T(8,128)} async-done(((f32[64,128,256]{2,1,0:T(8,128)}), f32[64,128,256]{2,1,0:T(8,128)}, u32[]{:S(2)}, u32[]{:S(2)}) %all-to-all-start.2) | async-done | bytes 8388640 | tf_op jit(solution)/shard_map/all_to_all | solution.py:173
  514.1 9.0 %copy.104 = f32[64,128,256]{1,2,0:T(8,128)} copy(f32[64,128,256]{2,1,0:T(8,128)} %all-to-all-done.2) | data formatting | bytes 16777216 | tf_op jit(solution)/shard_map/all_to_all | solution.py:173
  523.0 4.6 broadcast_multiply_fusion
  527.7 8.5 %fusion.24 = bf16[8,128,4,64]{1,0,3,2:T(8,128)(2,1)S(1)} fusion(f32[64,128,4,64]{1,3,2,0:T(8,128)S(1)} %broadcast_multiply_fusion, f32[8,4,64,128]{3,2,1,0:T(8,128)S(1)} %copy-done.3, f32[8,128,4]{1,0,2:T(8,128)S(1)} %convolution_add_fusion, f32[8,128,4]{1,0,2:T(8,128)S(1)} %get-tuple-element.189, s32[64]{0:T(128)S(1)} %copy-done.16, s32[8]{0:T(128)S(1)} %copy-done.13), kind=kOutput, calls=%fused_computation.36 | convolution fusion | flops 202375680 | bytes 9994528 | tf_op jit(solution)/shard_map/dg,dthe->gthe/dot_general | solution.py:185
  536.2 2.7 fusion.34
  538.9 153.4 %all-gather.3.cloned.1.call-done = f32[4096,1024]{1,0:T(8,128)} async-done(((f32[1024,1024]{1,0:T(8,128)}), f32[4096,1024]{1,0:T(8,128)}) %all-gather.3.cloned.1.call-update) | async-done | bytes 16777232 | tf_op jit(solution)/shard_map/all_gather | solution.py:196
  692.3 10.5 %reduce_sum.79 = f32[1024,1024]{1,0:T(8,128)} reduce(f32[4,1024,1024]{2,1,0:T(8,128)} %bitcast.145, f32[]{:T(128)} %constant.124.clone.1), dimensions={0}, to_apply=%region_11.12 | reduce | flops 3145728 | bytes 20971524 | tf_op jit(solution)/shard_map/reduce_sum | solution.py:197
  705.2 3.2 multiply_reduce_fusion
  (256 shorter events, 137.1 us)
Async XLA Ops:
  7.2 529.0 %copy-start = (bf16[256,1024]{1,0:T(8,128)(2,1)S(1)}, bf16[256,1024]{1,0:T(8,128)(2,1)}, u32[]{:S(2)}) copy-start(bf16[256,1024]{1,0:T(8,128)(2,1)} %param.30) | copy-start | bytes 1572868
  7.9 320.7 %copy-start.15 = (s32[64]{0:T(128)}, s32[64]{0:T(128)S(1)}, u32[]{:S(2)}) copy-start(s32[64]{0:T(128)S(1)} %and_select_fusion) | copy-start | bytes 772
  8.9 319.7 %copy-start.12 = (s32[8]{0:T(128)}, s32[8]{0:T(128)S(1)}, u32[]{:S(2)}) copy-start(s32[8]{0:T(128)S(1)} %slice_reduce_fusion) | copy-start | bytes 100
  9.0 23.9 %copy-start.17 = (pred[64]{0:T(512)(128)(4,1)}, pred[64]{0:T(512)(128)(4,1)S(1)}, u32[]{:S(2)}) copy-start(pred[64]{0:T(512)(128)(4,1)S(1)} %compare_and_fusion) | copy-start | bytes 196
  9.0 21.1 %copy-start.14 = (s32[1024]{0:T(1024)}, s32[1024]{0:T(1024)S(1)}, u32[]{:S(2)}) copy-start(s32[1024]{0:T(1024)S(1)} %pad_clamp_fusion) | copy-start | bytes 12292
  11.0 26.4 %all-to-all-start.1 = ((bf16[64,1,128]{2,1,0:T(2,128)(2,1)}), bf16[64,1,128]{2,1,0:T(2,128)(2,1)S(1)}, u32[]{:S(2)}, u32[]{:S(2)}) async-start(bf16[64,1,128]{2,1,0:T(2,128)(2,1)} %copy.100), calls=%async_computation.1 | async-start | bytes 65536 | tf_op jit(solution)/shard_map/all_to_all | solution.py:165
  24.9 4.8 copy-start.10
  37.4 10.7 %copy-start.26 = (s32[64]{0:T(128)S(1)}, s32[64]{0:T(128)}, u32[]{:S(2)}) copy-start(s32[64]{0:T(128)} %param.23) | copy-start | bytes 772
  37.4 13.9 %copy-start.6 = (bf16[512,256]{1,0:T(8,128)(2,1)S(1)}, bf16[512,256]{1,0:T(8,128)(2,1)}, u32[]{:S(2)}) copy-start(bf16[512,256]{1,0:T(8,128)(2,1)} %param.24) | copy-start | bytes 786436
  37.4 14.1 %copy-start.7 = (bf16[512,256]{1,0:T(8,128)(2,1)S(1)}, bf16[512,256]{1,0:T(8,128)(2,1)}, u32[]{:S(2)}) copy-start(bf16[512,256]{1,0:T(8,128)(2,1)} %param.25) | copy-start | bytes 786436
  37.4 14.3 %copy-start.27 = (s32[8]{0:T(128)S(1)}, s32[8]{0:T(128)}, u32[]{:S(2)}) copy-start(s32[8]{0:T(128)} %param.22) | copy-start | bytes 100
  37.4 14.9 %copy-start.23 = (f32[2,4]{1,0:T(2,128)S(1)}, f32[2,4]{1,0:T(2,128)}, u32[]{:S(2)}) copy-start(f32[2,4]{1,0:T(2,128)} %param.31) | copy-start | bytes 100
  37.4 106.5 %all-to-all-start = ((bf16[64,128,256]{2,1,0:T(8,128)(2,1)}), bf16[64,128,256]{2,1,0:T(8,128)(2,1)}, u32[]{:S(2)}, u32[]{:S(2)}) async-start(bf16[64,128,256]{2,1,0:T(8,128)(2,1)} %broadcast_select_fusion), calls=%async_computation | async-start | bytes 8388608 | tf_op jit(solution)/shard_map/all_to_all | solution.py:164
  156.9 12.7 %copy-start.8 = (s32[512]{0:T(512)S(1)}, s32[512]{0:T(512)}, u32[]{:S(2)}) copy-start(s32[512]{0:T(512)} %param.26) | copy-start | bytes 6148
  322.6 7.4 %copy-start.1 = (bf16[1024,1024]{1,0:T(8,128)(2,1)S(1)}, bf16[1024,1024]{1,0:T(8,128)(2,1)}, u32[]{:S(2)}) copy-start(bf16[1024,1024]{1,0:T(8,128)(2,1)} %param.18) | copy-start | bytes 6291460
  322.6 191.5 %all-to-all-start.2 = ((f32[64,128,256]{2,1,0:T(8,128)}), f32[64,128,256]{2,1,0:T(8,128)}, u32[]{:S(2)}, u32[]{:S(2)}) async-start(f32[64,128,256]{2,1,0:T(8,128)} %bitcast.147), calls=%async_computation.2 | async-start | bytes 16777216 | tf_op jit(solution)/shard_map/all_to_all | solution.py:173
  328.3 7.0 copy-start.9
  328.3 7.0 copy-start.2
  328.3 364.0 %all-gather.3.cloned.1.call-start = ((), (), s32[]{:S(2)}) async-start(), calls=%async_computation.5 | async-start | bytes 20971520 | tf_op jit(solution)/shard_map/all_gather | solution.py:196
  523.0 4.7 copy-start.3
  692.3 12.8 %copy-start.19 = (f32[1024]{0:T(1024)S(1)}, f32[1024]{0:T(1024)}, u32[]{:S(2)}) copy-start(f32[1024]{0:T(1024)} %param.33) | copy-start | bytes 12292
  692.3 12.8 %copy-start.20 = (f32[1024]{0:T(1024)S(1)}, f32[1024]{0:T(1024)}, u32[]{:S(2)}) copy-start(f32[1024]{0:T(1024)} %param.32) | copy-start | bytes 12292
  702.9 5.5 copy-start.11
  702.9 5.5 copy-start.22
  (8 other events, 10.8 us)
Sparse Core Ops, SparseCore 0:
  539.0 153.2 all-gather.2
